TPU v7x, 32 devices: a whole 2x2x4 slice. The times are simulated.
32 devices in a mesh: dp: 8 (over z, x), tensor: 4 (over y, core).
Axes of the slice: x: 2, y: 2, z: 4, core: 2. Of those that a mesh axis runs over, the one named last changes fastest.
Arguments:
- segments: bfloat16 [32, 704, 512], P('dp'), may hold values from -6 to 6
- seg_start: int32 [32, 704], P('dp'), may hold values from 0 to 2048, as said below
- seg_count: int32 [32], P('dp'), may hold values from 300 to 704, as said below
- norm_gain: bfloat16 [512], P('dp'), may hold values from 0.25 to 1.75
- norm_shift: bfloat16 [512], P('dp'), may hold values from -3 to 3
- qkv_weight: bfloat16 [512, 3, 512], P('dp', None, 'tensor'), may hold values from -0.25 to 0.25
- out_weight: bfloat16 [512, 512], P(('tensor', 'dp')), may hold values from -1 to 1
- ffn_gain: bfloat16 [512], P('dp'), may hold values from 0.25 to 1.75
- ffn_shift: bfloat16 [512], P('dp'), may hold values from -3 to 3
- up_weight: bfloat16 [512, 2048], P('dp', 'tensor'), may hold values from -0.25 to 0.25
- up_bias: bfloat16 [2048], P(('tensor', 'dp')), may hold values from -3 to 3
- down_weight: bfloat16 [2048, 512], P(('tensor', 'dp')), may hold values from -0.125 to 0.125
- cotangent: bfloat16 [32, 704, 512], P('dp'), may hold values from -6 to 6
Outputs:
- block_out: bfloat16 [32, 704, 512], P('dp')
- segments_grad: float32 [32, 704, 512], P('dp')
- norm_gain_grad: float32 [512], P('dp')
- norm_shift_grad: float32 [512], P('dp')
- qkv_weight_grad: float32 [512, 3, 512], P('dp', None, 'tensor')
- out_weight_grad: float32 [512, 512], P(('tensor', 'dp'))
- ffn_gain_grad: float32 [512], P('dp')
- ffn_shift_grad: float32 [512], P('dp')
- up_weight_grad: float32 [512, 2048], P('dp', 'tensor')
- up_bias_grad: float32 [2048], P(('tensor', 'dp'))
- down_weight_grad: float32 [2048, 512], P(('tensor', 'dp'))
Inputs may be any that keep to these rules, and one draw needn't show every extreme that they name: One sequence has exactly 704 live segments and one exactly 300; slots at and after seg_count are padding. `seg_start`: 0 in the first slot, strictly rising over a sequence's live segments and below 2048 there; 2048 in every padded slot.
All inputs are finite; a program needn't handle non-finite values.
Results may differ from a plain program's by a relative error of at most 0.014.
Values may be sent and summed in bfloat16 or wider, within the bound.
No kernel may reach another device: no remote copies, remote signals or barrier semaphores. Data moves between devices by JAX's collectives and lax.ppermute only.
A program may use at most 128 MiB of HBM per device.

v0:
```python
import math
import jax
import jax.numpy as jnp
from jax import lax
from jax.sharding import PartitionSpec as P

HEAD = 64
EPSILON = 1e-05
MASKED = -1e30


def split_up(array, dim, devices):
    dims = array.shape
    pieces = array.reshape(*dims[:dim], devices, dims[dim] // devices, *dims[dim + 1 :])
    return jnp.moveaxis(pieces, dim, 0)


def summed_on_arrival(array, axis, dim):
    pieces = split_up(array, dim, lax.axis_size(axis))
    arrived = lax.all_to_all(pieces, axis, split_axis=0, concat_axis=0, tiled=True)
    return arrived.astype(jnp.float32).sum(axis=0)


def sent_together(arrays, axis, dim, along):
    widths = [math.prod(a.shape[along:]) for a in arrays]
    both = jnp.concatenate(
        [a.reshape(*a.shape[:along], w) for a, w in zip(arrays, widths)], axis=along
    )
    filled = summed_on_arrival(both, axis, dim)
    pieces = jnp.split(filled, [sum(widths[:k]) for k in range(1, len(widths))], axis=along)
    return tuple(
        (b.reshape(*filled.shape[:along], *a.shape[along:]) for a, b in zip(arrays, pieces))
    )


def normalize(values, scale_vec, offset_vec):
    centre = jnp.mean(values, axis=-1, keepdims=True)
    centred = values - centre
    spread = jnp.mean(centred * centred, axis=-1, keepdims=True)
    return centred * lax.rsqrt(spread + EPSILON) * scale_vec + offset_vec


def rotate(values, cosine, sine_term):
    half_size = values.shape[-1] // 2
    turned = jnp.concatenate([-values[..., half_size:], values[..., :half_size]], axis=-1)
    return values * cosine + turned * sine_term


def rotary_tables(starts, head_size):
    half_size = head_size // 2
    freq_index = jnp.arange(half_size).astype(jnp.float32)
    inverse = jnp.exp(freq_index * (-math.log(10000.0) / half_size))
    angles = starts.astype(jnp.float32)[..., None] * inverse
    angles = jnp.concatenate([angles, angles], axis=-1)
    return (jnp.cos(angles), jnp.sin(angles))


def allowed_keys(length, live_count):
    places = jnp.arange(length)
    return (places[None, :] <= places[:, None]) & (places[None, :] < live_count)


def exact_gelu(values):
    return jax.nn.gelu(values, approximate=False)


def masked_scores(queries, key_rows, live_count):
    scores = jnp.einsum("qhd,khd->hqk", queries, key_rows, preferred_element_type=jnp.float32)
    allowed = allowed_keys(queries.shape[0], live_count)
    return jnp.where(allowed[None], scores, MASKED)


def attend_forward(packed):
    queries, key_rows, value_rows, live_count = packed
    scores = masked_scores(queries, key_rows, live_count)
    row_max = jnp.max(scores, axis=-1, keepdims=True)
    weights = jnp.exp(scores - row_max)
    row_total = jnp.sum(weights, axis=-1, keepdims=True)
    attention_probs = weights / row_total
    mixed_rows = jnp.einsum(
        "hqk,khd->qhd",
        attention_probs.astype(jnp.bfloat16),
        value_rows,
        preferred_element_type=jnp.float32,
    )
    return (mixed_rows.astype(jnp.bfloat16), row_max[..., 0] + jnp.log(row_total[..., 0]))


def attend_backward(packed):
    queries, key_rows, value_rows, live_count, log_total, out_grad = packed
    scores = masked_scores(queries, key_rows, live_count)
    attention_probs = jnp.exp(scores - log_total[..., None])
    prob_grad = jnp.einsum("qhd,khd->hqk", out_grad, value_rows, preferred_element_type=jnp.float32)
    inner_sum = jnp.sum(prob_grad * attention_probs, axis=-1, keepdims=True)
    score_grad = (attention_probs * (prob_grad - inner_sum)).astype(jnp.bfloat16)
    query_grad = jnp.einsum(
        "hqk,khd->qhd", score_grad, key_rows, preferred_element_type=jnp.float32
    )
    key_grad = jnp.einsum("hqk,qhd->khd", score_grad, queries, preferred_element_type=jnp.float32)
    value_grad = jnp.einsum(
        "hqk,qhd->khd",
        attention_probs.astype(jnp.bfloat16),
        out_grad,
        preferred_element_type=jnp.float32,
    )
    return (query_grad, key_grad, value_grad)


def run_layer(segments, seg_start, seg_count, cotangent, weights):
    seq_local, seg_len, model_width = segments.shape
    token_rows = seq_local * seg_len
    gain_one = weights[0].astype(jnp.float32)
    shift_one = weights[1].astype(jnp.float32)
    gain_two = weights[2].astype(jnp.float32)
    shift_two = weights[3].astype(jnp.float32)
    w_qkv, w_out, w_up = (weights[4], weights[5], weights[6])
    b_up = weights[7].astype(jnp.float32)
    w_down = weights[8]
    local_width = w_qkv.shape[2]
    local_heads = local_width // HEAD
    head_shape = (token_rows, local_heads, HEAD)
    seq_shape = (seq_local, seg_len, local_heads, HEAD)
    inputs = segments.reshape(token_rows, model_width).astype(jnp.float32)
    normed_one, norm_one_pull = jax.vjp(normalize, inputs, gain_one, shift_one)
    attn_in = normed_one.astype(jnp.bfloat16)
    projected = jnp.einsum("nd,dct->nct", attn_in, w_qkv, preferred_element_type=jnp.float32)
    cosine, sine_term = rotary_tables(seg_start.reshape(token_rows), HEAD)
    cosine = cosine[:, None, :]
    sine_term = sine_term[:, None, :]

    def place_rotary(raw_query, raw_key):
        return (
            rotate(raw_query, cosine, sine_term) * HEAD ** (-0.5),
            rotate(raw_key, cosine, sine_term),
        )

    rotated, rotary_pull = jax.vjp(
        place_rotary, projected[:, 0].reshape(head_shape), projected[:, 1].reshape(head_shape)
    )
    queries = rotated[0].astype(jnp.bfloat16).reshape(seq_shape)
    key_rows = rotated[1].astype(jnp.bfloat16).reshape(seq_shape)
    value_rows = projected[:, 2].astype(jnp.bfloat16).reshape(seq_shape)
    mixed_rows, log_total = lax.map(attend_forward, (queries, key_rows, value_rows, seg_count))
    mixed_flat = mixed_rows.reshape(token_rows, local_width)
    attn_part = jnp.dot(mixed_flat, w_out, preferred_element_type=jnp.float32)
    attn_full = lax.psum(attn_part, "tensor")
    residual = inputs + attn_full
    normed_two, norm_two_pull = jax.vjp(normalize, residual, gain_two, shift_two)
    ffn_in = normed_two.astype(jnp.bfloat16)
    pre_act = jnp.dot(ffn_in, w_up, preferred_element_type=jnp.float32) + b_up
    activated, gelu_pull = jax.vjp(exact_gelu, pre_act)
    act_low = activated.astype(jnp.bfloat16)
    ffn_part = jnp.dot(act_low, w_down, preferred_element_type=jnp.float32)
    ffn_full = lax.psum(ffn_part.astype(jnp.bfloat16), "tensor").astype(jnp.float32)
    block_out = (residual + ffn_full).astype(jnp.bfloat16).reshape(segments.shape)
    out_rows = cotangent.reshape(token_rows, model_width)
    down_grad = jnp.einsum("nf,nd->fd", act_low, out_rows, preferred_element_type=jnp.float32)
    act_grad = jnp.einsum("nd,fd->nf", out_rows, w_down, preferred_element_type=jnp.float32)
    pre_grad = gelu_pull(act_grad)[0].astype(jnp.bfloat16)
    bias_grad = jnp.sum(pre_grad, axis=0, dtype=jnp.float32)
    up_grad = jnp.einsum("nd,nf->df", ffn_in, pre_grad, preferred_element_type=jnp.float32)
    ffn_in_part = jnp.einsum("nf,df->nd", pre_grad, w_up, preferred_element_type=jnp.float32)
    ffn_in_grad = lax.psum(ffn_in_part, "tensor")
    resid_ln_grad, gain_two_grad, shift_two_grad = norm_two_pull(ffn_in_grad)
    residual_grad = out_rows.astype(jnp.float32) + resid_ln_grad
    attn_grad_low = residual_grad.astype(jnp.bfloat16)
    out_w_grad = jnp.einsum(
        "nt,nd->td", mixed_flat, attn_grad_low, preferred_element_type=jnp.float32
    )
    mixed_grad = jnp.einsum(
        "nd,td->nt", attn_grad_low, w_out, preferred_element_type=jnp.float32
    ).astype(jnp.bfloat16)
    ffn_shares = None
    query_grad, key_grad, value_grad = lax.map(
        attend_backward,
        (queries, key_rows, value_rows, seg_count, log_total, mixed_grad.reshape(seq_shape)),
    )
    raw_query_grad, raw_key_grad = rotary_pull(
        (query_grad.reshape(head_shape), key_grad.reshape(head_shape))
    )
    proj_grad = jnp.stack(
        [
            raw_query_grad.reshape(token_rows, local_width),
            raw_key_grad.reshape(token_rows, local_width),
            value_grad.reshape(token_rows, local_width),
        ],
        axis=1,
    ).astype(jnp.bfloat16)
    qkv_grad = jnp.einsum("nd,nct->dct", attn_in, proj_grad, preferred_element_type=jnp.float32)
    attn_in_part = jnp.einsum("nct,dct->nd", proj_grad, w_qkv, preferred_element_type=jnp.float32)
    attn_in_grad = lax.psum(attn_in_part.astype(jnp.bfloat16), "tensor").astype(jnp.float32)
    input_ln_grad, gain_one_grad, shift_one_grad = norm_one_pull(attn_in_grad)
    input_grad = (residual_grad + input_ln_grad).reshape(segments.shape)
    grads = (
        gain_one_grad,
        shift_one_grad,
        qkv_grad,
        out_w_grad,
        gain_two_grad,
        shift_two_grad,
        up_grad,
        bias_grad,
        down_grad,
    )
    return (block_out, input_grad, grads, ffn_shares)


def local(
    segments,
    seg_start,
    seg_count,
    norm_gain,
    norm_shift,
    qkv_weight,
    out_weight,
    ffn_gain,
    ffn_shift,
    up_weight,
    up_bias,
    down_weight,
    cotangent,
):
    gathered = (
        lax.all_gather(norm_gain, "dp", axis=0, tiled=True),
        lax.all_gather(norm_shift, "dp", axis=0, tiled=True),
        lax.all_gather(ffn_gain, "dp", axis=0, tiled=True),
        lax.all_gather(ffn_shift, "dp", axis=0, tiled=True),
        lax.all_gather(qkv_weight, "dp", axis=0, tiled=True),
        lax.all_gather(out_weight, "dp", axis=0, tiled=True),
        lax.all_gather(up_weight, "dp", axis=0, tiled=True),
        lax.all_gather(up_bias, "dp", axis=0, tiled=True),
        lax.all_gather(down_weight, "dp", axis=0, tiled=True),
    )
    block_out, input_grad, grads, ffn_shares = run_layer(
        segments, seg_start, seg_count, cotangent, gathered
    )
    (
        gain_one_grad,
        shift_one_grad,
        qkv_grad,
        out_w_grad,
        gain_two_grad,
        shift_two_grad,
        up_grad,
        bias_grad,
        down_grad,
    ) = grads
    shares = (
        summed_on_arrival(gain_one_grad.astype(jnp.bfloat16), "dp", 0),
        *sent_together(
            (shift_one_grad.astype(jnp.bfloat16), qkv_grad.astype(jnp.bfloat16)), "dp", 0, 1
        ),
        summed_on_arrival(out_w_grad.astype(jnp.bfloat16), "dp", 0),
        summed_on_arrival(gain_two_grad.astype(jnp.bfloat16), "dp", 0),
        *sent_together(
            (
                shift_two_grad.astype(jnp.bfloat16),
                up_grad.astype(jnp.bfloat16),
                bias_grad.astype(jnp.bfloat16),
                down_grad.astype(jnp.bfloat16),
            ),
            "dp",
            0,
            1,
        ),
    )
    gain_one_s, shift_one_s, qkv_s, out_s, gain_two_s, shift_two_s, up_s, bias_s, down_s = shares
    return (
        block_out,
        input_grad,
        gain_one_s,
        shift_one_s,
        qkv_s,
        out_s,
        gain_two_s,
        shift_two_s,
        up_s,
        bias_s,
        down_s,
    )


def solution(mesh):
    placed = (
        P("dp", None, None),
        P("dp", None),
        P("dp"),
        P("dp"),
        P("dp"),
        P("dp", None, "tensor"),
        P(("tensor", "dp"), None),
        P("dp"),
        P("dp"),
        P("dp", "tensor"),
        P(("tensor", "dp")),
        P(("tensor", "dp"), None),
        P("dp", None, None),
    )
    return jax.shard_map(
        local,
        mesh=mesh,
        in_specs=placed,
        out_specs=(
            P("dp", None, None),
            P("dp", None, None),
            P("dp"),
            P("dp"),
            P("dp", None, "tensor"),
            P(("tensor", "dp"), None),
            P("dp"),
            P("dp"),
            P("dp", "tensor"),
            P(("tensor", "dp")),
            P(("tensor", "dp"), None),
        ),
        check_vma=False,
    )
```

profile of v0, /device:TPU:0, one launch (start us, length us, event | category | flops | bytes accessed | tf_op | source)
XLA Modules:
  0.0 764.0 jit_solution(6756772383985416356)
XLA Ops:
  13.8 23.3 %all-reduce.9 = (bf16[512]{0:T(512)(128)(2,1)S(1)}, bf16[512]{0:T(512)(128)(2,1)S(1)}, bf16[512]{0:T(512)(128)(2,1)S(1)}, bf16[512]{0:T(512)(128)(2,1)S(1)}, bf16[512]{0:T(512)(128)(2,1)S(1)}) all-reduce(bf16[512]{0:T(512)(128)(2,1)S(1)} %dynamic-update-slice.1, ...), channel_id=1, replica_groups=mesh['dp'=8,'tensor'=4] {'dp'}, use_global_device_ids=true, to_apply=%add.5 | all-reduce | flops 2560 | bytes 10240
  37.3 31.0 %all_gather.29 = bf16[512,3,128]{2,0,1:T(8,128)(2,1)S(1)} all-gather(bf16[64,3,128]{2,0,1:T(8,128)(2,1)S(1)} %copy-done.44), channel_id=1, replica_groups=mesh['dp'=8,'tensor'=4] {'dp'}, dimensions={0}, use_global_device_ids=true | all-gather | bytes 442368 | tf_op jit(solution)/shard_map/all_gather | solution.py:228
  74.1 30.7 %all_gather.30 = bf16[128,512]{1,0:T(8,128)(2,1)S(1)} all-gather(bf16[16,512]{1,0:T(8,128)(2,1)S(1)} %copy-done.45), channel_id=1, replica_groups=mesh['dp'=8,'tensor'=4] {'dp'}, dimensions={0}, use_global_device_ids=true | all-gather | bytes 147456 | tf_op jit(solution)/shard_map/all_gather | solution.py:229
  104.9 6.5 fusion.85
  111.4 3.1 convert_element_type.201
  116.6 3.3 reshape_squeeze.10
  119.9 2.6 slice_negate_fusion.3
  122.5 2.6 concatenate.48
  125.1 2.7 concatenate.49
  127.8 3.3 reshape_squeeze.12
  133.7 2.6 concatenate.51
  136.3 2.6 concatenate.52
  138.9 4.0 fusion.78
  144.9 31.6 %while.26 = (s32[]{:T(128)}, bf16[4,704,2,64]{1,3,2,0:T(8,128)(2,1)}, f32[4,2,704]{2,1,0:T(2,128)}, bf16[4,704,2,64]{1,3,2,0:T(8,128)(2,1)}, s32[4]{0:T(128)S(1)...) while((s32[]{:T(128)}, bf16[4,704,2,64]{1,3,2,0:T(8,128)(2,1)}, ...), condition=%wide.region_5.6_spmd, body=%wide.region_2.5_spmd.sunk | while | flops 263757120 | bytes 14712817 | solution.py:143
  149.4 2.9 fusion.140
  157.3 2.9 fusion.140
  165.1 2.9 fusion.140
  173.0 3.0 fusion.140
  176.5 2.6 copy.92
  179.1 2.7 reshape.398
  181.9 4.6 fusion.97
  188.4 31.8 %all_gather.33 = bf16[512,512]{1,0:T(8,128)(2,1)S(1)} all-gather(bf16[64,512]{1,0:T(8,128)(2,1)} %param.26), channel_id=1, replica_groups=mesh['dp'=8,'tensor'=4] {'dp'}, dimensions={0}, use_global_device_ids=true | all-gather | bytes 589824 | tf_op jit(solution)/shard_map/all_gather | solution.py:230
  220.2 33.4 %all_gather.35 = bf16[512,512]{1,0:T(8,128)(2,1)} all-gather(bf16[64,512]{1,0:T(8,128)(2,1)} %param.28), channel_id=1, replica_groups=mesh['dp'=8,'tensor'=4] {'dp'}, dimensions={0}, use_global_device_ids=true | all-gather | bytes 589824 | tf_op jit(solution)/shard_map/all_gather | solution.py:232
  253.5 41.4 %all-reduce.15.cloned.1.call-done = f32[2816,512]{1,0:T(8,128)} async-done(((f32[2816,512]{1,0:T(8,128)}), f32[2816,512]{1,0:T(8,128)}) %all-reduce.15.cloned.1.call-update) | async-done | bytes 5767184 | tf_op jit(solution)/shard_map/psum | solution.py:146
  295.0 3.3 fusion.92
  303.4 16.5 %fusion.89 = (bf16[512]{0:T(512)(128)(2,1)}, bf16[2816,512]{1,0:T(8,128)(2,1)S(1)}, f32[2816,512]{1,0:T(8,128)}) fusion(f32[2816,512]{1,0:T(8,128)S(1)} %fusion.98, f32[512]{0:T(512)S(1)} %copy-done.48, bf16[2816,512]{1,0:T(8,128)(2,1)S(1)} %bitcast.198, bf16[512,512]{1,0:T(8,128)(2,1)S(1)} %copy-done.29), kind=kOutput, calls=%fused_computation.166 | convolution fusion | flops 1583087104 | bytes 17828864 | tf_op jit(solution)/shard_map/nd,fd->nf/dot_general | solution.py:158
  321.4 4.1 fusion.99
  326.4 3.8 broadcast_multiply_fusion.3
  330.1 7.0 multiply_convert_fusion.1
  337.2 3.3 convolution_convert_fusion
  343.1 93.9 %all-reduce.17.cloned.1.call-done = f32[2816,512]{1,0:T(8,128)} async-done(((f32[2816,512]{1,0:T(8,128)}), f32[2816,512]{1,0:T(8,128)}) %all-reduce.17.cloned.1.call-update) | async-done | bytes 5767184 | tf_op jit(solution)/shard_map/psum | solution.py:163
  437.0 6.3 multiply_reduce_fusion.1
  443.3 6.5 fusion.91
  450.4 5.5 all-to-all-start.3
  456.0 3.3 fusion.69
  463.4 3.4 copy.96
  466.9 106.9 %while.27 = (s32[]{:T(128)}, f32[4,704,2,64]{1,0,3,2:T(4,128)}, f32[4,704,2,64]{1,0,3,2:T(4,128)}, bf16[4,704,2,64]{1,3,2,0:T(8,128)(2,1)}, bf16[4,704,2,64]{1,3...) while((s32[]{:T(128)}, f32[4,704,2,64]{1,0,3,2:T(4,128)}, ...), condition=%wide.region_15.16_spmd, body=%wide.region_13.15_spmd.sunk | while | flops 647273792 | bytes 44077144 | solution.py:174
  471.0 2.5 multiply_reduce_fusion.5
  476.8 8.4 %dynamic_update_slice.30 = f32[4,704,2,64]{1,0,3,2:T(4,128)} dynamic-update-slice(f32[4,704,2,64]{1,0,3,2:T(4,128)} %get-tuple-element.440, f32[1,704,2,64]{1,0,3,2:T(1,128)S(1)} %copy.151, s32[]{:T(128)S(6)} %copy.177, s32[]{:T(128)} %constant.60.clone.1..sunk, s32[]{:T(128)} %constant.60.clone.1..sunk, s32[]{:T(128)} %constant.60.clone.1..sunk) | dynamic-update-slice | bytes 720900 | tf_op jit(solution)/shard_map/while/body/jit(dynamic_update_index_in_dim)/dynamic_update_slice | solution.py:174
  485.2 8.4 %dynamic_update_slice.29 = f32[4,704,2,64]{1,0,3,2:T(4,128)} dynamic-update-slice(f32[4,704,2,64]{1,0,3,2:T(4,128)} %get-tuple-element.439, f32[1,704,2,64]{1,0,3,2:T(1,128)S(1)} %copy.150, s32[]{:T(128)S(6)} %copy.177, s32[]{:T(128)} %constant.60.clone.1..sunk, s32[]{:T(128)} %constant.60.clone.1..sunk, s32[]{:T(128)} %constant.60.clone.1..sunk) | dynamic-update-slice | bytes 720900 | tf_op jit(solution)/shard_map/while/body/jit(dynamic_update_index_in_dim)/dynamic_update_slice | solution.py:174
  497.8 2.5 multiply_reduce_fusion.5
  503.5 8.4 %dynamic_update_slice.30 = f32[4,704,2,64]{1,0,3,2:T(4,128)} dynamic-update-slice(f32[4,704,2,64]{1,0,3,2:T(4,128)} %get-tuple-element.440, f32[1,704,2,64]{1,0,3,2:T(1,128)S(1)} %copy.151, s32[]{:T(128)S(6)} %copy.177, s32[]{:T(128)} %constant.60.clone.1..sunk, s32[]{:T(128)} %constant.60.clone.1..sunk, s32[]{:T(128)} %constant.60.clone.1..sunk) | dynamic-update-slice | bytes 720900 | tf_op jit(solution)/shard_map/while/body/jit(dynamic_update_index_in_dim)/dynamic_update_slice | solution.py:174
  511.9 8.4 %dynamic_update_slice.29 = f32[4,704,2,64]{1,0,3,2:T(4,128)} dynamic-update-slice(f32[4,704,2,64]{1,0,3,2:T(4,128)} %get-tuple-element.439, f32[1,704,2,64]{1,0,3,2:T(1,128)S(1)} %copy.150, s32[]{:T(128)S(6)} %copy.177, s32[]{:T(128)} %constant.60.clone.1..sunk, s32[]{:T(128)} %constant.60.clone.1..sunk, s32[]{:T(128)} %constant.60.clone.1..sunk) | dynamic-update-slice | bytes 720900 | tf_op jit(solution)/shard_map/while/body/jit(dynamic_update_index_in_dim)/dynamic_update_slice | solution.py:174
  530.2 8.4 %dynamic_update_slice.30 = f32[4,704,2,64]{1,0,3,2:T(4,128)} dynamic-update-slice(f32[4,704,2,64]{1,0,3,2:T(4,128)} %get-tuple-element.440, f32[1,704,2,64]{1,0,3,2:T(1,128)S(1)} %copy.151, s32[]{:T(128)S(6)} %copy.177, s32[]{:T(128)} %constant.60.clone.1..sunk, s32[]{:T(128)} %constant.60.clone.1..sunk, s32[]{:T(128)} %constant.60.clone.1..sunk) | dynamic-update-slice | bytes 720900 | tf_op jit(solution)/shard_map/while/body/jit(dynamic_update_index_in_dim)/dynamic_update_slice | solution.py:174
  538.6 8.4 %dynamic_update_slice.29 = f32[4,704,2,64]{1,0,3,2:T(4,128)} dynamic-update-slice(f32[4,704,2,64]{1,0,3,2:T(4,128)} %get-tuple-element.439, f32[1,704,2,64]{1,0,3,2:T(1,128)S(1)} %copy.150, s32[]{:T(128)S(6)} %copy.177, s32[]{:T(128)} %constant.60.clone.1..sunk, s32[]{:T(128)} %constant.60.clone.1..sunk, s32[]{:T(128)} %constant.60.clone.1..sunk) | dynamic-update-slice | bytes 720900 | tf_op jit(solution)/shard_map/while/body/jit(dynamic_update_index_in_dim)/dynamic_update_slice | solution.py:174
  556.9 8.4 %dynamic_update_slice.30 = f32[4,704,2,64]{1,0,3,2:T(4,128)} dynamic-update-slice(f32[4,704,2,64]{1,0,3,2:T(4,128)} %get-tuple-element.440, f32[1,704,2,64]{1,0,3,2:T(1,128)S(1)} %copy.151, s32[]{:T(128)S(6)} %copy.177, s32[]{:T(128)} %constant.60.clone.1..sunk, s32[]{:T(128)} %constant.60.clone.1..sunk, s32[]{:T(128)} %constant.60.clone.1..sunk) | dynamic-update-slice | bytes 720900 | tf_op jit(solution)/shard_map/while/body/jit(dynamic_update_index_in_dim)/dynamic_update_slice | solution.py:174
  565.3 8.4 %dynamic_update_slice.29 = f32[4,704,2,64]{1,0,3,2:T(4,128)} dynamic-update-slice(f32[4,704,2,64]{1,0,3,2:T(4,128)} %get-tuple-element.439, f32[1,704,2,64]{1,0,3,2:T(1,128)S(1)} %copy.150, s32[]{:T(128)S(6)} %copy.177, s32[]{:T(128)} %constant.60.clone.1..sunk, s32[]{:T(128)} %constant.60.clone.1..sunk, s32[]{:T(128)} %constant.60.clone.1..sunk) | dynamic-update-slice | bytes 720900 | tf_op jit(solution)/shard_map/while/body/jit(dynamic_update_index_in_dim)/dynamic_update_slice | solution.py:174
  573.8 3.9 copy.119
  582.8 2.6 reshape.403
  593.0 4.5 bitcast_convert_fusion
  601.6 6.0 all-to-all-start.2
  607.6 5.2 convolution_convert_fusion.2
  615.4 3.5 concatenate.60
  619.0 6.0 all-to-all-start.4
  625.0 3.2 fusion.79
  631.7 20.8 %all-to-all-done.4 = bf16[8,64,1026]{2,1,0:T(8,128)(2,1)} async-done(((bf16[8,64,1026]{2,1,0:T(8,128)(2,1)}), bf16[8,64,1026]{2,1,0:T(8,128)(2,1)}, u32[]{:S(2)}, u32[]{:S(2)}) %all-to-all-start.4) | async-done | bytes 1050656 | tf_op jit(solution)/shard_map/all_to_all | solution.py:20
  655.6 54.0 %all-reduce.19.cloned.1.call-done = (bf16[2816,512]{1,0:T(8,128)(2,1)}, bf16[2816,512]{1,0:T(8,128)(2,1)}) async-done(((bf16[2816,512]{1,0:T(8,128)(2,1)}, bf16[2816,512]{1,0:T(8,128)(2,1)}), (bf16[2816,512]{1,0:T(8,128)(2,1)}, bf16[2816,512]{1,0:T(8,128)(2,1)})) %all-reduce.19.cloned.1.call-update) | async-done | bytes 5767184 | tf_op jit(solution)/shard_map/psum | solution.py:154
  709.6 3.4 fusion.53
  715.2 4.8 fusion.54
  720.7 5.8 all-to-all-start
  726.5 8.1 %add_add_fusion.2 = f32[2816,512]{1,0:T(8,128)} fusion(bf16[4,704,512]{2,1,0:T(8,128)(2,1)S(1)} %copy-done.2, bf16[2816,512]{1,0:T(8,128)(2,1)} %get-tuple-element.256, f32[2816,512]{1,0:T(8,128)} %get-tuple-element.261, f32[2816]{0:T(1024)S(1)} %negate_multiply_fusion.1, f32[2816]{0:T(1024)S(1)} %multiply_multiply_fusion.5, ...), kind=kLoop, calls=%fused_computation.83 | loop fusion | flops 18743296 | bytes 20243456 | tf_op jit(solution)/shard_map/add | solution.py:193
  736.0 6.0 all-to-all-start.1
  742.0 6.1 add_convert_fusion.1
  748.6 7.1 all-to-all-done.1
  (290 shorter events, 120.8 us)
Async XLA Ops:
  7.2 4.1 copy-start.58
  7.2 2.7 copy-start.1
  7.2 5.3 copy-start.51
  7.2 5.6 copy-start.52
  7.2 5.8 copy-start.53
  7.2 6.1 copy-start.54
  7.2 6.3 copy-start.55
  7.3 30.0 %copy-start.44 = (bf16[64,3,128]{2,0,1:T(8,128)(2,1)S(1)}, bf16[64,3,128]{2,0,1:T(8,128)(2,1)}, u32[]{:S(2)}) copy-start(bf16[64,3,128]{2,0,1:T(8,128)(2,1)} %param.22) | copy-start | bytes 147460
  7.3 287.7 %all-reduce.15.cloned.1.call-start = ((), (), s32[]{:S(2)}) async-start(), calls=%async_computation.5 | async-start | bytes 11534336 | tf_op jit(solution)/shard_map/psum | solution.py:146
  7.3 97.5 %copy-start.49 = (f32[32]{0:T(128)}, f32[32]{0:T(128)S(1)}, u32[]{:S(2)}) copy-start(f32[32]{0:T(128)S(1)} %multiply_exponential_fusion) | copy-start | bytes 388
  9.9 60.0 %copy-start.31 = (f32[2816]{0:T(1024)}, f32[2816]{0:T(1024)S(1)}, u32[]{:S(2)}) copy-start(f32[2816]{0:T(1024)S(1)} %div.47) | copy-start | bytes 33796
  37.1 34.2 %copy-start.41 = (f32[512]{0:T(512)}, f32[512]{0:T(512)S(1)}, u32[]{:S(2)}) copy-start(f32[512]{0:T(512)S(1)} %convert_element_type.198) | copy-start | bytes 6148
  37.3 34.1 %copy-start.37 = (f32[2816]{0:T(1024)}, f32[2816]{0:T(1024)S(1)}, u32[]{:S(2)}) copy-start(f32[2816]{0:T(1024)S(1)} %add.103) | copy-start | bytes 33796
  37.3 31.1 %copy-start.33 = (f32[2816]{0:T(1024)}, f32[2816]{0:T(1024)S(1)}, u32[]{:S(2)}) copy-start(f32[2816]{0:T(1024)S(1)} %rsqrt.20) | copy-start | bytes 33796
  68.3 3.0 copy-start.22
  69.9 2.4 copy-start.11
  71.3 2.7 copy-start.46
  71.4 2.7 copy-start.45
  138.9 6.0 copy-start.56
  186.5 250.5 %all-reduce.17.cloned.1.call-start = ((), (), s32[]{:S(2)}) async-start(), calls=%async_computation.6 | async-start | bytes 11534336 | tf_op jit(solution)/shard_map/psum | solution.py:163
  298.3 3.2 copy-start
  299.4 2.1 copy-start.39
  299.4 2.1 copy-start.35
  301.5 1.8 copy-start.9
  301.5 1.9 copy-start.29
  301.5 1.9 copy-start.48
  303.2 16.7 %copy-start.5 = (f32[2816,512]{1,0:T(8,128)}, f32[2816,512]{1,0:T(8,128)S(1)}, u32[]{:S(2)}) copy-start(f32[2816,512]{1,0:T(8,128)S(1)} %fusion.98) | copy-start | bytes 17301508
  330.1 7.0 copy-start.30
  337.2 3.3 copy-start.20
  337.2 3.5 copy-start.14
  340.6 96.4 %copy-start.36 = (f32[2816]{0:T(1024)S(1)}, f32[2816]{0:T(1024)}, u32[]{:S(2)}) copy-start(f32[2816]{0:T(1024)} %copy-done.35) | copy-start | bytes 33796
  343.1 100.2 %copy-start.40 = (f32[2816]{0:T(1024)S(1)}, f32[2816]{0:T(1024)}, u32[]{:S(2)}) copy-start(f32[2816]{0:T(1024)} %copy-done.39) | copy-start | bytes 33796
  437.0 6.3 copy-start.6
  443.3 12.7 %copy-start.10 = (bf16[4,704,512]{2,1,0:T(8,128)(2,1)S(1)}, bf16[4,704,512]{2,1,0:T(8,128)(2,1)}, u32[]{:S(2)}) copy-start(bf16[4,704,512]{2,1,0:T(8,128)(2,1)} %param.29) | copy-start | bytes 8650756
  450.4 151.2 %all-to-all-start.3 = ((bf16[8,1,64]{2,1,0:T(2,128)(2,1)}), bf16[8,1,64]{2,1,0:T(2,128)(2,1)S(1)}, u32[]{:S(2)}, u32[]{:S(2)}) async-start(bf16[8,1,64]{2,1,0:T(2,128)(2,1)} %convert_element_type.240), calls=%async_computation.3 | async-start | bytes 8192 | tf_op jit(solution)/shard_map/all_to_all | solution.py:20
  456.0 253.6 %all-reduce.19.cloned.1.call-start = ((), (), s32[]{:S(2)}) async-start(), calls=%async_computation.7 | async-start | bytes 11534336 | tf_op jit(solution)/shard_map/psum | solution.py:154
  460.9 5.9 copy-start.7
  460.9 5.9 copy-start.8
  460.9 5.9 copy-start.57
  466.9 3.0 copy-start.24
  471.0 2.5 copy-start.25
  493.6 3.0 copy-start.24
  497.8 2.5 copy-start.25
  520.4 3.0 copy-start.24
  524.5 2.5 copy-start.25
  547.1 3.0 copy-start.24
  551.2 2.5 copy-start.25
  573.8 7.7 %copy-start.15 = (f32[2816,64]{0,1:T(8,128)S(1)}, f32[2816,64]{0,1:T(8,128)}, u32[]{:S(2)}) copy-start(f32[2816,64]{0,1:T(8,128)} %get-tuple-element.283) | copy-start | bytes 2162692
  585.4 1.7 copy-start.18
  585.4 2.0 copy-start.19
  587.3 5.7 copy-start.23
  597.5 1.8 copy-start.4
  601.6 17.4 %all-to-all-start.2 = ((bf16[8,16,512]{2,1,0:T(8,128)(2,1)}), bf16[8,16,512]{2,1,0:T(8,128)(2,1)}, u32[]{:S(2)}, u32[]{:S(2)}) async-start(bf16[8,16,512]{2,1,0:T(8,128)(2,1)} %bitcast.31), calls=%async_computation.2 | async-start | bytes 262144 | tf_op jit(solution)/shard_map/all_to_all | solution.py:20
  607.5 7.9 %copy-start.28 = (bf16[512,512]{1,0:T(8,128)(2,1)S(1)}, bf16[512,512]{1,0:T(8,128)(2,1)}, u32[]{:S(2)}) copy-start(bf16[512,512]{1,0:T(8,128)(2,1)} %convolution_convert_fusion.3) | copy-start | bytes 1572868
  612.8 12.2 %copy-start.12 = (bf16[2816,512]{1,0:T(8,128)(2,1)S(1)}, bf16[2816,512]{1,0:T(8,128)(2,1)}, u32[]{:S(2)}) copy-start(bf16[2816,512]{1,0:T(8,128)(2,1)} %copy-done.11) | copy-start | bytes 8650756
  619.0 33.6 %all-to-all-start.4 = ((bf16[8,64,1026]{2,1,0:T(8,128)(2,1)}), bf16[8,64,1026]{2,1,0:T(8,128)(2,1)}, u32[]{:S(2)}, u32[]{:S(2)}) async-start(bf16[8,64,1026]{2,1,0:T(8,128)(2,1)} %concatenate.60), calls=%async_computation.4 | async-start | bytes 2359296 | tf_op jit(solution)/shard_map/all_to_all | solution.py:20
  624.9 84.6 %copy-start.32 = (f32[2816]{0:T(1024)S(1)}, f32[2816]{0:T(1024)}, u32[]{:S(2)}) copy-start(f32[2816]{0:T(1024)} %copy-done.31) | copy-start | bytes 33796
  625.0 84.6 %copy-start.42 = (f32[512]{0:T(512)S(1)}, f32[512]{0:T(512)}, u32[]{:S(2)}) copy-start(f32[512]{0:T(512)} %copy-done.41) | copy-start | bytes 6148
  628.2 81.4 %copy-start.2 = (bf16[4,704,512]{2,1,0:T(8,128)(2,1)S(1)}, bf16[4,704,512]{2,1,0:T(8,128)(2,1)}, u32[]{:S(2)}) copy-start(bf16[4,704,512]{2,1,0:T(8,128)(2,1)} %param.17) | copy-start | bytes 8650756
  709.6 5.7 copy-start.38
  709.6 5.7 copy-start.34
  720.7 15.3 %all-to-all-start = ((bf16[8,1,64]{2,1,0:T(2,128)(2,1)}), bf16[8,1,64]{2,1,0:T(2,128)(2,1)S(1)}, u32[]{:S(2)}, u32[]{:S(2)}) async-start(bf16[8,1,64]{2,1,0:T(2,128)(2,1)} %convert_element_type.238), calls=%async_computation | async-start | bytes 8192 | tf_op jit(solution)/shard_map/all_to_all | solution.py:20
  726.5 8.3 %copy-start.21 = (bf16[8,64,384]{2,1,0:T(8,128)(2,1)S(1)}, bf16[8,64,384]{2,1,0:T(8,128)(2,1)}, u32[]{:S(2)}) copy-start(bf16[8,64,384]{2,1,0:T(8,128)(2,1)} %concatenate.55) | copy-start | bytes 1179652
  736.0 19.8 %all-to-all-start.1 = ((bf16[8,64,385]{2,1,0:T(8,128)(2,1)}), bf16[8,64,385]{2,1,0:T(8,128)(2,1)S(1)}, u32[]{:S(2)}, u32[]{:S(2)}) async-start(bf16[8,64,385]{2,1,0:T(8,128)(2,1)} %pad_maximum_fusion.5), calls=%async_computation.1 | async-start | bytes 1048576 | tf_op jit(solution)/shard_map/all_to_all | solution.py:20
  (9 other events, 11.3 us)
Sparse Core Ops, SparseCore 0:
  186.6 108.3 all-reduce.14
  325.7 111.2 all-reduce.16
  597.6 111.8 all-reduce.18
where the time goes:
time: 773 us; the launch traced here: 764 us
  waiting for transfers between devices  217 us (28%)
  local copies, waits for them, and re-layouts  151 us (20%)
  blocking collectives  150 us (19%)
  other arithmetic  107 us (14%)
  matrix products  92.4 us (12%)
  starting transfers between devices  29.4 us (4%)
  between operations  15.5 us (2%)
    psum x1, waiting for transfers between devices, run_layer(): ffn_in_grad = lax.psum(ffn_in_part, 'tensor')  93.9 us
    dynamic_update_slice x16, local copies, waits for them, and re-layouts, run_layer(): lax.map(attend_backward, (queries, key_rows, value_rows, seg_count, log_t...  70.8 us
    psum x1, waiting for transfers between devices, run_layer(): lax.psum(ffn_part.astype(jnp.bfloat16), 'tensor').astype(jnp.float32)  54 us
    psum x1, waiting for transfers between devices, run_layer(): attn_full = lax.psum(attn_part, 'tensor')  41.4 us
    all_gather x1, blocking collectives, local(): lax.all_gather(down_weight, 'dp', axis=0, tiled=True)  33.4 us
    all_gather x1, blocking collectives, local(): lax.all_gather(up_weight, 'dp', axis=0, tiled=True)  31.8 us
    all_gather x1, blocking collectives, local(): lax.all_gather(qkv_weight, 'dp', axis=0, tiled=True)  31 us
    all_gather x1, blocking collectives, local(): lax.all_gather(out_weight, 'dp', axis=0, tiled=True)  30.7 us
  transfers between devices with their start and end apart: 8, of which 5 were waited for; matrix products, arithmetic and copies ran while one was open for 26% of the time, Pallas kernels for 0%

commit v1 on v0

--- a/solution.py
+++ b/solution.py
@@ -160,7 +160,11 @@
     bias_grad = jnp.sum(pre_grad, axis=0, dtype=jnp.float32)
     up_grad = jnp.einsum("nd,nf->df", ffn_in, pre_grad, preferred_element_type=jnp.float32)
     ffn_in_part = jnp.einsum("nf,df->nd", pre_grad, w_up, preferred_element_type=jnp.float32)
-    ffn_in_grad = lax.psum(ffn_in_part, "tensor")
+    ffn_in_grad = ffn_in_part
+    for hop in (1, 2):
+        ffn_in_grad = ffn_in_grad + lax.ppermute(
+            ffn_in_grad, "tensor", [(dev, dev ^ hop) for dev in range(4)]
+        )
     resid_ln_grad, gain_two_grad, shift_two_grad = norm_two_pull(ffn_in_grad)
     residual_grad = out_rows.astype(jnp.float32) + resid_ln_grad
     attn_grad_low = residual_grad.astype(jnp.bfloat16)

time: 773 us -> 803 us (1.039)
  waiting for transfers between devices: 217 us -> 244 us
    ppermute x0 -> x2, waiting for transfers between devices: none -> 120 us  [run_layer(): lax.ppermute(ffn_in_grad, 'tensor', [(dev, dev ^ hop) for dev in range(4)])]
    psum x1 -> x0, waiting for transfers between devices: 93.9 us -> none  [run_layer(): ffn_in_grad = lax.psum(ffn_in_part, 'tensor')]
  transfers between devices with their start and end apart: 8 -> 9, of which waited for: 5 -> 6; matrix products, arithmetic and copies ran while one was open for 26% -> 25% of each run, Pallas kernels for 0% -> 0%
where the time goes in v1:
time: 803 us; the launch traced here: 795 us
  waiting for transfers between devices  244 us (30%)
  local copies, waits for them, and re-layouts  152 us (19%)
  blocking collectives  150 us (19%)
  other arithmetic  110 us (14%)
  matrix products  92 us (11%)
  starting transfers between devices  30 us (4%)
  between operations  15.8 us (2%)
    ppermute x2, waiting for transfers between devices, run_layer(): lax.ppermute(ffn_in_grad, 'tensor', [(dev, dev ^ hop) for dev in range(4)])  120 us
    dynamic_update_slice x16, local copies, waits for them, and re-layouts, run_layer(): lax.map(attend_backward, (queries, key_rows, value_rows, seg_count, log_t...  70.7 us
    psum x1, waiting for transfers between devices, run_layer(): lax.psum(ffn_part.astype(jnp.bfloat16), 'tensor').astype(jnp.float32)  54.3 us
    psum x1, waiting for transfers between devices, run_layer(): attn_full = lax.psum(attn_part, 'tensor')  42.2 us
    all_gather x1, blocking collectives, local(): lax.all_gather(down_weight, 'dp', axis=0, tiled=True)  33.4 us
    all_gather x1, blocking collectives, local(): lax.all_gather(up_weight, 'dp', axis=0, tiled=True)  31.8 us
    all_gather x1, blocking collectives, local(): lax.all_gather(qkv_weight, 'dp', axis=0, tiled=True)  31 us
    all_gather x1, blocking collectives, local(): lax.all_gather(out_weight, 'dp', axis=0, tiled=True)  30.7 us
  transfers between devices with their start and end apart: 9, of which 6 were waited for; matrix products, arithmetic and copies ran while one was open for 25% of the time, Pallas kernels for 0%

profile of v1, /device:TPU:0, one launch (start us, length us, event | category | flops | bytes accessed | tf_op | source)
XLA Modules:
  0.0 794.6 jit_solution(2069515532452653294)
XLA Ops:
  9.9 3.0 fusion.62
  15.5 23.3 %all-reduce.9 = (bf16[512]{0:T(512)(128)(2,1)S(1)}, bf16[512]{0:T(512)(128)(2,1)S(1)}, bf16[512]{0:T(512)(128)(2,1)S(1)}, bf16[512]{0:T(512)(128)(2,1)S(1)}, bf16[512]{0:T(512)(128)(2,1)S(1)}) all-reduce(bf16[512]{0:T(512)(128)(2,1)S(1)} %dynamic-update-slice.1, ...), channel_id=1, replica_groups=mesh['dp'=8,'tensor'=4] {'dp'}, use_global_device_ids=true, to_apply=%add.5 | all-reduce | flops 2560 | bytes 10240
  39.0 31.0 %all_gather.29 = bf16[512,3,128]{2,0,1:T(8,128)(2,1)S(1)} all-gather(bf16[64,3,128]{2,0,1:T(8,128)(2,1)S(1)} %copy-done.42), channel_id=1, replica_groups=mesh['dp'=8,'tensor'=4] {'dp'}, dimensions={0}, use_global_device_ids=true | all-gather | bytes 442368 | tf_op jit(solution)/shard_map/all_gather | solution.py:232
  77.4 30.7 %all_gather.30 = bf16[128,512]{1,0:T(8,128)(2,1)S(1)} all-gather(bf16[16,512]{1,0:T(8,128)(2,1)S(1)} %copy-done.43), channel_id=1, replica_groups=mesh['dp'=8,'tensor'=4] {'dp'}, dimensions={0}, use_global_device_ids=true | all-gather | bytes 147456 | tf_op jit(solution)/shard_map/all_gather | solution.py:233
  108.2 6.4 fusion.85
  114.6 3.1 convert_element_type.201
  119.9 3.3 reshape_squeeze.10
  123.2 2.5 slice_negate_fusion.3
  125.7 2.6 concatenate.48
  128.4 2.7 concatenate.49
  131.1 3.3 reshape_squeeze.12
  136.9 2.6 concatenate.51
  139.5 2.6 concatenate.52
  142.2 4.0 fusion.78
  148.2 31.6 %while.26 = (s32[]{:T(128)}, bf16[4,704,2,64]{1,3,2,0:T(8,128)(2,1)}, f32[4,2,704]{2,1,0:T(2,128)}, bf16[4,704,2,64]{1,3,2,0:T(8,128)(2,1)}, s32[4]{0:T(128)S(1)...) while((s32[]{:T(128)}, bf16[4,704,2,64]{1,3,2,0:T(8,128)(2,1)}, ...), condition=%wide.region_5.6_spmd, body=%wide.region_2.5_spmd.sunk | while | flops 263757120 | bytes 14712817 | solution.py:143
  152.7 2.9 fusion.140
  160.5 2.9 fusion.140
  168.4 2.9 fusion.140
  176.2 2.9 fusion.140
  179.8 2.6 copy.92
  182.4 2.7 reshape.398
  185.1 4.6 fusion.97
  190.9 31.8 %all_gather.33 = bf16[512,512]{1,0:T(8,128)(2,1)S(1)} all-gather(bf16[64,512]{1,0:T(8,128)(2,1)} %param.26), channel_id=1, replica_groups=mesh['dp'=8,'tensor'=4] {'dp'}, dimensions={0}, use_global_device_ids=true | all-gather | bytes 589824 | tf_op jit(solution)/shard_map/all_gather | solution.py:234
  222.7 33.4 %all_gather.35 = bf16[512,512]{1,0:T(8,128)(2,1)} all-gather(bf16[64,512]{1,0:T(8,128)(2,1)} %param.28), channel_id=1, replica_groups=mesh['dp'=8,'tensor'=4] {'dp'}, dimensions={0}, use_global_device_ids=true | all-gather | bytes 589824 | tf_op jit(solution)/shard_map/all_gather | solution.py:236
  256.1 42.2 %all-reduce.14.cloned.1.call-done = f32[2816,512]{1,0:T(8,128)} async-done(((f32[2816,512]{1,0:T(8,128)}), f32[2816,512]{1,0:T(8,128)}) %all-reduce.14.cloned.1.call-update) | async-done | bytes 5767184 | tf_op jit(solution)/shard_map/psum | solution.py:146
  298.2 3.3 fusion.92
  307.8 16.5 %fusion.89 = (bf16[512]{0:T(512)(128)(2,1)}, bf16[2816,512]{1,0:T(8,128)(2,1)S(1)}, f32[2816,512]{1,0:T(8,128)}) fusion(f32[2816,512]{1,0:T(8,128)S(1)} %fusion.98, f32[512]{0:T(512)S(1)} %copy-done.46, bf16[2816,512]{1,0:T(8,128)(2,1)S(1)} %bitcast.200, bf16[512,512]{1,0:T(8,128)(2,1)S(1)} %copy-done.26), kind=kOutput, calls=%fused_computation.166 | convolution fusion | flops 1583087104 | bytes 17828864 | tf_op jit(solution)/shard_map/nd,fd->nf/dot_general | solution.py:158
  327.6 9.4 %collective-permute-done = f32[2816,512]{1,0:T(8,128)S(1)} collective-permute-done((f32[2816,512]{1,0:T(8,128)S(1)}, f32[2816,512]{1,0:T(8,128)S(1)}, u32[]{:S(2)}, u32[]{:S(2)}) %collective-permute-start) | collective-permute-done | bytes 5767200 | tf_op jit(solution)/shard_map/ppermute | solution.py:165
  337.0 3.9 add.119
  341.7 3.8 broadcast_multiply_fusion.3
  345.4 6.0 multiply_convert_fusion.1
  351.5 3.3 convolution_convert_fusion
  357.3 110.3 %collective-permute-done.1 = f32[2816,512]{1,0:T(8,128)} collective-permute-done((f32[2816,512]{1,0:T(8,128)}, f32[2816,512]{1,0:T(8,128)}, u32[]{:S(2)}, u32[]{:S(2)}) %collective-permute-start.1) | collective-permute-done | bytes 5767200 | tf_op jit(solution)/shard_map/ppermute | solution.py:165
  467.6 6.5 multiply_reduce_fusion.1
  474.2 4.3 fusion.91
  479.2 5.5 all-to-all-start.3
  484.7 3.3 fusion.69
  492.1 3.4 copy.96
  495.6 108.5 %while.27 = (s32[]{:T(128)}, f32[4,704,2,64]{1,0,3,2:T(4,128)}, f32[4,704,2,64]{1,0,3,2:T(4,128)}, bf16[4,704,2,64]{1,3,2,0:T(8,128)(2,1)}, bf16[4,704,2,64]{1,3...) while((s32[]{:T(128)}, f32[4,704,2,64]{1,0,3,2:T(4,128)}, ...), condition=%wide.region_14.15_spmd, body=%wide.region_12.14_spmd.sunk | while | flops 647273792 | bytes 38309920 | solution.py:178
  505.8 8.4 %dynamic_update_slice.30 = f32[4,704,2,64]{1,0,3,2:T(4,128)} dynamic-update-slice(f32[4,704,2,64]{1,0,3,2:T(4,128)} %get-tuple-element.441, f32[1,704,2,64]{1,0,3,2:T(1,128)S(1)} %copy.151, s32[]{:T(128)S(6)} %copy.176, s32[]{:T(128)} %constant.60.clone.1..sunk, s32[]{:T(128)} %constant.60.clone.1..sunk, s32[]{:T(128)} %constant.60.clone.1..sunk) | dynamic-update-slice | bytes 720900 | tf_op jit(solution)/shard_map/while/body/jit(dynamic_update_index_in_dim)/dynamic_update_slice | solution.py:178
  514.3 8.4 %dynamic_update_slice.29 = f32[4,704,2,64]{1,0,3,2:T(4,128)} dynamic-update-slice(f32[4,704,2,64]{1,0,3,2:T(4,128)} %get-tuple-element.440, f32[1,704,2,64]{1,0,3,2:T(1,128)S(1)} %copy.150, s32[]{:T(128)S(6)} %copy.176, s32[]{:T(128)} %constant.60.clone.1..sunk, s32[]{:T(128)} %constant.60.clone.1..sunk, s32[]{:T(128)} %constant.60.clone.1..sunk) | dynamic-update-slice | bytes 720900 | tf_op jit(solution)/shard_map/while/body/jit(dynamic_update_index_in_dim)/dynamic_update_slice | solution.py:178
  533.0 8.4 %dynamic_update_slice.30 = f32[4,704,2,64]{1,0,3,2:T(4,128)} dynamic-update-slice(f32[4,704,2,64]{1,0,3,2:T(4,128)} %get-tuple-element.441, f32[1,704,2,64]{1,0,3,2:T(1,128)S(1)} %copy.151, s32[]{:T(128)S(6)} %copy.176, s32[]{:T(128)} %constant.60.clone.1..sunk, s32[]{:T(128)} %constant.60.clone.1..sunk, s32[]{:T(128)} %constant.60.clone.1..sunk) | dynamic-update-slice | bytes 720900 | tf_op jit(solution)/shard_map/while/body/jit(dynamic_update_index_in_dim)/dynamic_update_slice | solution.py:178
  541.4 8.4 %dynamic_update_slice.29 = f32[4,704,2,64]{1,0,3,2:T(4,128)} dynamic-update-slice(f32[4,704,2,64]{1,0,3,2:T(4,128)} %get-tuple-element.440, f32[1,704,2,64]{1,0,3,2:T(1,128)S(1)} %copy.150, s32[]{:T(128)S(6)} %copy.176, s32[]{:T(128)} %constant.60.clone.1..sunk, s32[]{:T(128)} %constant.60.clone.1..sunk, s32[]{:T(128)} %constant.60.clone.1..sunk) | dynamic-update-slice | bytes 720900 | tf_op jit(solution)/shard_map/while/body/jit(dynamic_update_index_in_dim)/dynamic_update_slice | solution.py:178
  560.1 8.4 %dynamic_update_slice.30 = f32[4,704,2,64]{1,0,3,2:T(4,128)} dynamic-update-slice(f32[4,704,2,64]{1,0,3,2:T(4,128)} %get-tuple-element.441, f32[1,704,2,64]{1,0,3,2:T(1,128)S(1)} %copy.151, s32[]{:T(128)S(6)} %copy.176, s32[]{:T(128)} %constant.60.clone.1..sunk, s32[]{:T(128)} %constant.60.clone.1..sunk, s32[]{:T(128)} %constant.60.clone.1..sunk) | dynamic-update-slice | bytes 720900 | tf_op jit(solution)/shard_map/while/body/jit(dynamic_update_index_in_dim)/dynamic_update_slice | solution.py:178
  568.5 8.4 %dynamic_update_slice.29 = f32[4,704,2,64]{1,0,3,2:T(4,128)} dynamic-update-slice(f32[4,704,2,64]{1,0,3,2:T(4,128)} %get-tuple-element.440, f32[1,704,2,64]{1,0,3,2:T(1,128)S(1)} %copy.150, s32[]{:T(128)S(6)} %copy.176, s32[]{:T(128)} %constant.60.clone.1..sunk, s32[]{:T(128)} %constant.60.clone.1..sunk, s32[]{:T(128)} %constant.60.clone.1..sunk) | dynamic-update-slice | bytes 720900 | tf_op jit(solution)/shard_map/while/body/jit(dynamic_update_index_in_dim)/dynamic_update_slice | solution.py:178
  587.2 8.4 %dynamic_update_slice.30 = f32[4,704,2,64]{1,0,3,2:T(4,128)} dynamic-update-slice(f32[4,704,2,64]{1,0,3,2:T(4,128)} %get-tuple-element.441, f32[1,704,2,64]{1,0,3,2:T(1,128)S(1)} %copy.151, s32[]{:T(128)S(6)} %copy.176, s32[]{:T(128)} %constant.60.clone.1..sunk, s32[]{:T(128)} %constant.60.clone.1..sunk, s32[]{:T(128)} %constant.60.clone.1..sunk) | dynamic-update-slice | bytes 720900 | tf_op jit(solution)/shard_map/while/body/jit(dynamic_update_index_in_dim)/dynamic_update_slice | solution.py:178
  595.6 8.4 %dynamic_update_slice.29 = f32[4,704,2,64]{1,0,3,2:T(4,128)} dynamic-update-slice(f32[4,704,2,64]{1,0,3,2:T(4,128)} %get-tuple-element.440, f32[1,704,2,64]{1,0,3,2:T(1,128)S(1)} %copy.150, s32[]{:T(128)S(6)} %copy.176, s32[]{:T(128)} %constant.60.clone.1..sunk, s32[]{:T(128)} %constant.60.clone.1..sunk, s32[]{:T(128)} %constant.60.clone.1..sunk) | dynamic-update-slice | bytes 720900 | tf_op jit(solution)/shard_map/while/body/jit(dynamic_update_index_in_dim)/dynamic_update_slice | solution.py:178
  604.1 3.9 copy.119
  613.1 2.6 reshape.403
  623.3 4.5 bitcast_convert_fusion
  631.9 6.1 all-to-all-start.2
  638.0 5.3 convolution_convert_fusion.2
  645.8 3.5 concatenate.60
  649.3 6.0 all-to-all-start.4
  655.3 3.2 fusion.79
  662.1 20.5 %all-to-all-done.4 = bf16[8,64,1026]{2,1,0:T(8,128)(2,1)} async-done(((bf16[8,64,1026]{2,1,0:T(8,128)(2,1)}), bf16[8,64,1026]{2,1,0:T(8,128)(2,1)}, u32[]{:S(2)}, u32[]{:S(2)}) %all-to-all-start.4) | async-done | bytes 1050656 | tf_op jit(solution)/shard_map/all_to_all | solution.py:20
  685.6 54.3 %all-reduce.16.cloned.1.call-done = (bf16[2816,512]{1,0:T(8,128)(2,1)}, bf16[2816,512]{1,0:T(8,128)(2,1)}) async-done(((bf16[2816,512]{1,0:T(8,128)(2,1)}, bf16[2816,512]{1,0:T(8,128)(2,1)}), (bf16[2816,512]{1,0:T(8,128)(2,1)}, bf16[2816,512]{1,0:T(8,128)(2,1)})) %all-reduce.16.cloned.1.call-update) | async-done | bytes 5767184 | tf_op jit(solution)/shard_map/psum | solution.py:154
  739.9 3.3 fusion.53
  745.5 4.8 fusion.54
  751.0 5.8 all-to-all-start
  756.8 8.1 %add_add_fusion.2 = f32[2816,512]{1,0:T(8,128)} fusion(bf16[4,704,512]{2,1,0:T(8,128)(2,1)S(1)} %copy-done.2, bf16[2816,512]{1,0:T(8,128)(2,1)} %get-tuple-element.256, f32[2816,512]{1,0:T(8,128)} %get-tuple-element.261, f32[2816]{0:T(1024)S(1)} %negate_multiply_fusion.1, f32[2816]{0:T(1024)S(1)} %multiply_multiply_fusion.5, ...), kind=kLoop, calls=%fused_computation.83 | loop fusion | flops 18743296 | bytes 20243456 | tf_op jit(solution)/shard_map/add | solution.py:197
  766.3 6.0 all-to-all-start.1
  772.3 6.1 add_convert_fusion.1
  778.9 7.1 all-to-all-done.1
  (281 shorter events, 129.6 us)
Async XLA Ops:
  7.2 5.8 copy-start.56
  7.2 62.8 %copy-start.1 = (bf16[4,704,512]{2,1,0:T(8,128)(2,1)S(1)}, bf16[4,704,512]{2,1,0:T(8,128)(2,1)}, u32[]{:S(2)}) copy-start(bf16[4,704,512]{2,1,0:T(8,128)(2,1)} %param.17) | copy-start | bytes 8650756
  7.2 7.0 copy-start.49
  7.2 7.3 copy-start.50
  7.2 7.5 copy-start.51
  7.2 7.8 copy-start.52
  7.2 8.0 %copy-start.53 = (bf16[64]{0:T(256)(128)(2,1)S(1)}, bf16[64]{0:T(256)(128)(2,1)}, u32[]{:S(2)}) copy-start(bf16[64]{0:T(256)(128)(2,1)} %param.27) | copy-start | bytes 388
  7.3 31.7 %copy-start.42 = (bf16[64,3,128]{2,0,1:T(8,128)(2,1)S(1)}, bf16[64,3,128]{2,0,1:T(8,128)(2,1)}, u32[]{:S(2)}) copy-start(bf16[64,3,128]{2,0,1:T(8,128)(2,1)} %param.22) | copy-start | bytes 147460
  7.3 291.0 %all-reduce.14.cloned.1.call-start = ((), (), s32[]{:S(2)}) async-start(), calls=%async_computation.5 | async-start | bytes 11534336 | tf_op jit(solution)/shard_map/psum | solution.py:146
  7.3 100.7 %copy-start.47 = (f32[32]{0:T(128)}, f32[32]{0:T(128)S(1)}, u32[]{:S(2)}) copy-start(f32[32]{0:T(128)S(1)} %multiply_exponential_fusion) | copy-start | bytes 388
  9.9 64.7 %copy-start.28 = (f32[2816]{0:T(1024)}, f32[2816]{0:T(1024)S(1)}, u32[]{:S(2)}) copy-start(f32[2816]{0:T(1024)S(1)} %div.47) | copy-start | bytes 33796
  38.8 35.8 %copy-start.40 = (f32[512]{0:T(512)}, f32[512]{0:T(512)S(1)}, u32[]{:S(2)}) copy-start(f32[512]{0:T(512)S(1)} %convert_element_type.198) | copy-start | bytes 6148
  38.9 35.7 %copy-start.36 = (f32[2816]{0:T(1024)}, f32[2816]{0:T(1024)S(1)}, u32[]{:S(2)}) copy-start(f32[2816]{0:T(1024)S(1)} %add.107) | copy-start | bytes 33796
  39.0 31.1 %copy-start.30 = (f32[2816]{0:T(1024)}, f32[2816]{0:T(1024)S(1)}, u32[]{:S(2)}) copy-start(f32[2816]{0:T(1024)S(1)} %rsqrt.20) | copy-start | bytes 33796
  70.0 4.6 copy-start.21
  71.6 1.6 copy-start.10
  73.2 4.1 copy-start.44
  73.2 4.1 copy-start.43
  77.4 51.0 %copy-start.34 = (f32[4,704]{1,0:T(4,128)}, f32[4,704]{1,0:T(4,128)S(1)}, u32[]{:S(2)}) copy-start(f32[4,704]{1,0:T(4,128)S(1)} %convert_element_type.202) | copy-start | bytes 33796
  142.2 6.0 copy-start.54
  301.5 4.3 copy-start
  301.5 2.3 copy-start.45
  302.6 4.9 copy-start.38
  305.8 1.8 copy-start.8
  305.9 1.9 copy-start.26
  305.9 1.9 copy-start.46
  307.5 16.8 %copy-start.5 = (f32[2816,512]{1,0:T(8,128)}, f32[2816,512]{1,0:T(8,128)S(1)}, u32[]{:S(2)}) copy-start(f32[2816,512]{1,0:T(8,128)S(1)} %fusion.98) | copy-start | bytes 17301508
  327.5 14.0 %copy-start.35 = (f32[4,704]{1,0:T(4,128)S(1)}, f32[4,704]{1,0:T(4,128)}, u32[]{:S(2)}) copy-start(f32[4,704]{1,0:T(4,128)} %copy-done.34) | copy-start | bytes 33796
  327.5 14.0 %copy-start.48 = (f32[32]{0:T(128)S(1)}, f32[32]{0:T(128)}, u32[]{:S(2)}) copy-start(f32[32]{0:T(128)} %copy-done.47) | copy-start | bytes 388
  327.5 9.5 %collective-permute-start = (f32[2816,512]{1,0:T(8,128)S(1)}, f32[2816,512]{1,0:T(8,128)S(1)}, u32[]{:S(2)}, u32[]{:S(2)}) collective-permute-start(f32[2816,512]{1,0:T(8,128)S(1)} %fusion.99), channel_id=1, source_target_pairs={{0,1},{1,0},{2,3},{3,2},{4,5},{5,4},{6,7},{7,6},{8,9},{9,8},{10,11... | collective-permute-start | bytes 17301512 | tf_op jit(solution)/shard_map/ppermute | solution.py:165
  341.0 126.6 %collective-permute-start.1 = (f32[2816,512]{1,0:T(8,128)}, f32[2816,512]{1,0:T(8,128)}, u32[]{:S(2)}, u32[]{:S(2)}) collective-permute-start(f32[2816,512]{1,0:T(8,128)} %add.119), channel_id=1, source_target_pairs={{0,2},{1,3},{2,0},{3,1},{4,6},{5,7},{6,4},{7,5},{8,10},{9,11},{10,... | collective-permute-start | bytes 17301512 | tf_op jit(solution)/shard_map/ppermute | solution.py:165
  345.4 6.0 copy-start.27
  345.4 122.2 %slice-start = ((s8[5767168]{0:T(1024)(128)(4,1)}), s8[1572864]{0:T(1024)(128)(4,1)S(1)}, s32[]{:S(2)}) async-start(s8[5767168]{0:T(1024)(128)(4,1)} %bitcast.195), calls=%async_computation.7 | async-start | bytes 3145728
  351.5 3.3 copy-start.19
  351.5 3.3 copy-start.13
  351.5 116.1 %slice-start.1 = ((s8[5767168]{0:T(1024)(128)(4,1)}), s8[4194304]{0:T(1024)(128)(4,1)S(1)}, s32[]{:S(2)}) async-start(s8[5767168]{0:T(1024)(128)(4,1)} %bitcast.195), calls=%async_computation.8 | async-start | bytes 8388608
  354.8 112.8 %copy-start.33 = (f32[2816]{0:T(1024)S(1)}, f32[2816]{0:T(1024)}, u32[]{:S(2)}) copy-start(f32[2816]{0:T(1024)} %copy-done.32) | copy-start | bytes 33796
  357.3 116.9 %copy-start.39 = (f32[2816]{0:T(1024)S(1)}, f32[2816]{0:T(1024)}, u32[]{:S(2)}) copy-start(f32[2816]{0:T(1024)} %copy-done.38) | copy-start | bytes 33796
  474.1 10.5 %copy-start.9 = (bf16[4,704,512]{2,1,0:T(8,128)(2,1)S(1)}, bf16[4,704,512]{2,1,0:T(8,128)(2,1)}, u32[]{:S(2)}) copy-start(bf16[4,704,512]{2,1,0:T(8,128)(2,1)} %param.29) | copy-start | bytes 8650756
  479.2 152.7 %all-to-all-start.3 = ((bf16[8,1,64]{2,1,0:T(2,128)(2,1)}), bf16[8,1,64]{2,1,0:T(2,128)(2,1)S(1)}, u32[]{:S(2)}, u32[]{:S(2)}) async-start(bf16[8,1,64]{2,1,0:T(2,128)(2,1)} %convert_element_type.240), calls=%async_computation.3 | async-start | bytes 8192 | tf_op jit(solution)/shard_map/all_to_all | solution.py:20
  484.6 255.2 %all-reduce.16.cloned.1.call-start = ((), (), s32[]{:S(2)}) async-start(), calls=%async_computation.6 | async-start | bytes 11534336 | tf_op jit(solution)/shard_map/psum | solution.py:154
  488.0 1.6 copy-start.3
  489.6 5.9 copy-start.6
  489.6 5.9 copy-start.7
  489.6 6.0 copy-start.55
  604.1 7.7 copy-start.14
  615.6 1.5 copy-start.16
  615.6 1.7 copy-start.17
  615.7 2.0 copy-start.18
  617.6 5.7 copy-start.22
  620.7 1.7 copy-start.23
  627.8 1.8 copy-start.4
  631.9 13.9 %copy-start.25 = (bf16[512,512]{1,0:T(8,128)(2,1)S(1)}, bf16[512,512]{1,0:T(8,128)(2,1)}, u32[]{:S(2)}) copy-start(bf16[512,512]{1,0:T(8,128)(2,1)} %convolution_convert_fusion.3) | copy-start | bytes 1572868
  631.9 17.4 %all-to-all-start.2 = ((bf16[8,16,512]{2,1,0:T(8,128)(2,1)}), bf16[8,16,512]{2,1,0:T(8,128)(2,1)}, u32[]{:S(2)}, u32[]{:S(2)}) async-start(bf16[8,16,512]{2,1,0:T(8,128)(2,1)} %bitcast.31), calls=%async_computation.2 | async-start | bytes 262144 | tf_op jit(solution)/shard_map/all_to_all | solution.py:20
  638.0 17.3 %copy-start.11 = (bf16[2816,512]{1,0:T(8,128)(2,1)S(1)}, bf16[2816,512]{1,0:T(8,128)(2,1)}, u32[]{:S(2)}) copy-start(bf16[2816,512]{1,0:T(8,128)(2,1)} %copy-done.10) | copy-start | bytes 8650756
  649.3 33.3 %all-to-all-start.4 = ((bf16[8,64,1026]{2,1,0:T(8,128)(2,1)}), bf16[8,64,1026]{2,1,0:T(8,128)(2,1)}, u32[]{:S(2)}, u32[]{:S(2)}) async-start(bf16[8,64,1026]{2,1,0:T(8,128)(2,1)} %concatenate.60), calls=%async_computation.4 | async-start | bytes 2359296 | tf_op jit(solution)/shard_map/all_to_all | solution.py:20
  655.3 84.6 %copy-start.29 = (f32[2816]{0:T(1024)S(1)}, f32[2816]{0:T(1024)}, u32[]{:S(2)}) copy-start(f32[2816]{0:T(1024)} %copy-done.28) | copy-start | bytes 33796
  655.3 84.5 %copy-start.41 = (f32[512]{0:T(512)S(1)}, f32[512]{0:T(512)}, u32[]{:S(2)}) copy-start(f32[512]{0:T(512)} %copy-done.40) | copy-start | bytes 6148
  658.6 81.3 %copy-start.2 = (bf16[4,704,512]{2,1,0:T(8,128)(2,1)S(1)}, bf16[4,704,512]{2,1,0:T(8,128)(2,1)}, u32[]{:S(2)}) copy-start(bf16[4,704,512]{2,1,0:T(8,128)(2,1)} %param.17) | copy-start | bytes 8650756
  658.9 86.6 %copy-start.37 = (f32[2816]{0:T(1024)S(1)}, f32[2816]{0:T(1024)}, u32[]{:S(2)}) copy-start(f32[2816]{0:T(1024)} %copy-done.36) | copy-start | bytes 33796
  658.9 86.6 %copy-start.31 = (f32[2816]{0:T(1024)S(1)}, f32[2816]{0:T(1024)}, u32[]{:S(2)}) copy-start(f32[2816]{0:T(1024)} %copy-done.30) | copy-start | bytes 33796
  751.0 15.3 %all-to-all-start = ((bf16[8,1,64]{2,1,0:T(2,128)(2,1)}), bf16[8,1,64]{2,1,0:T(2,128)(2,1)S(1)}, u32[]{:S(2)}, u32[]{:S(2)}) async-start(bf16[8,1,64]{2,1,0:T(2,128)(2,1)} %convert_element_type.238), calls=%async_computation | async-start | bytes 8192 | tf_op jit(solution)/shard_map/all_to_all | solution.py:20
  756.8 8.3 %copy-start.20 = (bf16[8,64,384]{2,1,0:T(8,128)(2,1)S(1)}, bf16[8,64,384]{2,1,0:T(8,128)(2,1)}, u32[]{:S(2)}) copy-start(bf16[8,64,384]{2,1,0:T(8,128)(2,1)} %concatenate.55) | copy-start | bytes 1179652
  766.3 19.8 %all-to-all-start.1 = ((bf16[8,64,385]{2,1,0:T(8,128)(2,1)}), bf16[8,64,385]{2,1,0:T(8,128)(2,1)S(1)}, u32[]{:S(2)}, u32[]{:S(2)}) async-start(bf16[8,64,385]{2,1,0:T(8,128)(2,1)} %pad_maximum_fusion.5), calls=%async_computation.1 | async-start | bytes 1048576 | tf_op jit(solution)/shard_map/all_to_all | solution.py:20
  (4 other events, 5.1 us)
Sparse Core Ops, SparseCore 0:
  189.8 108.3 all-reduce.13
  627.9 111.9 all-reduce.15
